TPU v7x, 32 devices: a whole 2x2x4 slice. The times are simulated.
32 devices in a mesh: groups: 2 (over y), row: 16 (over z, x, core).
Axes of the slice: x: 2, y: 2, z: 4, core: 2. Of those that a mesh axis runs over, the one named last changes fastest.
Arguments:
- layer_input: bfloat16 [8192, 512], P('row', 'groups'), parts along dimension 1, may hold values from -6 to 6
- output_grad: bfloat16 [8192, 512], P('row', 'groups'), parts along dimension 1, may hold values from -1.5 to 1.5
- gate_weight: bfloat16 [28672, 8192], P(('groups', 'row')), parts along dimension 0, may hold values from -0.09375 to 0.09375
- up_weight: bfloat16 [28672, 8192], P(('groups', 'row')), parts along dimension 0, may hold values from -0.09375 to 0.09375
- down_weight: bfloat16 [28672, 8192], P(('groups', 'row')), parts along dimension 0, may hold values from -0.046875 to 0.046875
Outputs:
- input_grad: bfloat16 [8192, 512], P('row', 'groups'), parts along dimension 1
- gate_grad: bfloat16 [28672, 8192], P(('groups', 'row')), parts along dimension 0
- up_grad: bfloat16 [28672, 8192], P(('groups', 'row')), parts along dimension 0
- down_grad: bfloat16 [28672, 8192], P(('groups', 'row')), parts along dimension 0
There are 2 independent parts, one for each index of `groups`. A program takes and returns all parts, laid end to end along the dimension named above; each array names one. Nothing has to cross between parts.
All inputs are finite; a program needn't handle non-finite values.
Results may differ from a plain program's by a relative error of at most 0.0049.
Values may be sent and summed in bfloat16 or wider, within the bound.
A program may use at most 192 MiB of HBM per device.

v0:
```python
import jax
import jax.numpy as jnp
from jax import lax
from jax.sharding import PartitionSpec as P


def over_tokens(first_mat, second_mat):
    return lax.dot_general(
        first_mat, second_mat, (((1,), (1,)), ((), ())), preferred_element_type=jnp.float32
    )


def over_hidden(first_mat, second_mat):
    return lax.dot_general(
        first_mat, second_mat, (((0,), (0,)), ((), ())), preferred_element_type=jnp.float32
    )


def activation_parts(gate_pre, up_pre):
    sig = jax.nn.sigmoid(gate_pre)
    act = gate_pre * sig
    hidden_act = (act * up_pre).astype(jnp.bfloat16)
    return (sig, act, hidden_act)


def pre_grads(hidden_grad, gate_pre, up_pre, sig, act):
    grad_gate_pre = (hidden_grad * up_pre * sig * (1.0 + gate_pre * (1.0 - sig))).astype(
        jnp.bfloat16
    )
    grad_up_pre = (hidden_grad * act).astype(jnp.bfloat16)
    return (grad_gate_pre, grad_up_pre)


def on_device(layer_input, output_grad, gate_weight, up_weight, down_weight):
    block_in = lax.all_gather(layer_input, "row", axis=0, tiled=True)
    gate_pre = jnp.dot(gate_weight, block_in, preferred_element_type=jnp.float32)
    up_pre = jnp.dot(up_weight, block_in, preferred_element_type=jnp.float32)
    sig, act, hidden_act = activation_parts(gate_pre, up_pre)
    block_in = lax.all_gather(output_grad, "row", axis=0, tiled=True)
    grad_new = jnp.dot(down_weight, block_in, preferred_element_type=jnp.float32)
    grad_block = over_tokens(hidden_act, block_in).astype(jnp.bfloat16)
    grad_gate_pre, grad_up_pre = pre_grads(grad_new, gate_pre, up_pre, sig, act)
    block_in = lax.all_gather(layer_input, "row", axis=0, tiled=True)
    gate_grad = over_tokens(grad_gate_pre, block_in).astype(jnp.bfloat16)
    up_grad = over_tokens(grad_up_pre, block_in).astype(jnp.bfloat16)
    terms = over_hidden(gate_weight, grad_gate_pre) + over_hidden(up_weight, grad_up_pre)
    input_grad = lax.psum_scatter(terms, "row", scatter_dimension=0, tiled=True).astype(
        jnp.bfloat16
    )
    return (input_grad, gate_grad, up_grad, grad_block)


def solution(mesh):
    return jax.shard_map(
        on_device,
        mesh=mesh,
        in_specs=(
            P("row", "groups"),
            P("row", "groups"),
            P(("groups", "row"), None),
            P(("groups", "row"), None),
            P(("groups", "row"), None),
        ),
        out_specs=(
            P("row", "groups"),
            P(("groups", "row"), None),
            P(("groups", "row"), None),
            P(("groups", "row"), None),
        ),
        check_vma=False,
    )
```

profile of v0, /device:TPU:14, one launch (start us, length us, event | category | flops | bytes accessed | tf_op | source)
XLA Modules:
  0.0 254.8 jit_solution(9589781873817059000)
XLA Ops:
  7.2 0.0 all-gather.5.cloned.1.call-start
  7.2 0.7 all-gather.5.cloned.1.call-update
  7.9 0.0 all-gather.3.cloned.1.call-start
  7.9 0.7 all-gather.3.cloned.1.call-update
  8.6 0.0 reduce-scatter.2.cloned.1.call-start
  8.7 52.1 %all-gather.5.cloned.1.call-done = bf16[8192,256]{1,0:T(8,128)(2,1)} async-done(((bf16[512,256]{1,0:T(8,128)(2,1)}), bf16[8192,256]{1,0:T(8,128)(2,1)}) %all-gather.5.cloned.1.call-update) | async-done | bytes 4194320 | tf_op jit(solution)/shard_map/all_gather | solution.py:35
  60.8 0.0 copy-start
  60.8 0.0 copy-start.1
  60.8 8.6 %fusion.5 = f32[896,256]{1,0:T(8,128)S(1)} fusion(bf16[896,8192]{1,0:T(8,128)(2,1)} %param.7, bf16[8192,256]{1,0:T(8,128)(2,1)} %all-gather.5.cloned.1.call-done), kind=kOutput, calls=%fused_computation.12 | convolution fusion | flops 3758096384 | bytes 19791872 | tf_op jit(solution)/shard_map/dot_general | solution.py:36
  69.4 2.1 copy-done
  71.5 1.3 copy-done.1
  72.8 3.9 %fusion.4 = f32[896,256]{1,0:T(8,128)S(1)} fusion(bf16[896,8192]{1,0:T(8,128)(2,1)S(1)} %copy-done, bf16[8192,256]{1,0:T(8,128)(2,1)S(1)} %copy-done.1), kind=kOutput, calls=%fused_computation.11 | convolution fusion | flops 3758096384 | bytes 19791872 | tf_op jit(solution)/shard_map/dot_general | solution.py:37
  76.7 35.1 %all-gather.3.cloned.1.call-done = bf16[8192,256]{1,0:T(8,128)(2,1)} async-done(((bf16[512,256]{1,0:T(8,128)(2,1)}), bf16[8192,256]{1,0:T(8,128)(2,1)}) %all-gather.3.cloned.1.call-update) | async-done | bytes 4194320 | tf_op jit(solution)/shard_map/all_gather | solution.py:39
  111.9 10.5 %multiply_convert_fusion.1 = (bf16[896,256]{1,0:T(8,128)(2,1)S(1)}, bf16[896,256]{1,0:T(8,128)(2,1)S(1)}) fusion(f32[896,256]{1,0:T(8,128)S(1)} %fusion.5, f32[896,256]{1,0:T(8,128)S(1)} %fusion.4, bf16[896,8192]{1,0:T(8,128)(2,1)} %param.9, bf16[8192,256]{1,0:T(8,128)(2,1)} %all-gather.3.cloned.1.call-done), kind=kOutput, calls=%fused_computation.6 | convolution fusion | flops 3761078272 | bytes 21626880 | tf_op jit(solution)/shard_map/dot_general | solution.py:40
  122.4 8.0 %fusion.6 = f32[256,8192]{1,0:T(8,128)S(1)} fusion(bf16[896,256]{1,0:T(8,128)(2,1)S(1)} %get-tuple-element.9, bf16[896,8192]{1,0:T(8,128)(2,1)} %param.7), kind=kOutput, calls=%fused_computation.13 | convolution fusion | flops 3758096384 | bytes 23527424 | tf_op jit(solution)/shard_map/dot_general | solution.py:14
  130.4 12.5 %fusion = f32[8192,256]{0,1:T(8,128)} fusion(f32[256,8192]{1,0:T(8,128)S(1)} %fusion.6, bf16[896,256]{1,0:T(8,128)(2,1)S(1)} %get-tuple-element.8, bf16[896,8192]{1,0:T(8,128)(2,1)} %param.8), kind=kOutput, calls=%fused_computation.4 | convolution fusion | flops 3760193536 | bytes 31916032 | tf_op jit(solution)/shard_map/dot_general | solution.py:14
  142.9 0.0 reduce-scatter.2.cloned.1.call-update
  143.0 10.5 %convolution_convert_fusion.1 = bf16[896,8192]{1,0:T(8,128)(2,1)} fusion(bf16[896,256]{1,0:T(8,128)(2,1)S(1)} %get-tuple-element.8, bf16[8192,256]{1,0:T(8,128)(2,1)} %all-gather.5.cloned.1.call-done), kind=kOutput, calls=%fused_computation.1 | convolution fusion | flops 3765436416 | bytes 19333120 | tf_op jit(solution)/shard_map/dot_general | solution.py:8
  153.5 10.8 %convolution_convert_fusion.2 = bf16[896,8192]{1,0:T(8,128)(2,1)} fusion(bf16[896,256]{1,0:T(8,128)(2,1)S(1)} %get-tuple-element.9, bf16[8192,256]{1,0:T(8,128)(2,1)} %all-gather.5.cloned.1.call-done), kind=kOutput, calls=%fused_computation.2 | convolution fusion | flops 3765436416 | bytes 19333120 | tf_op jit(solution)/shard_map/dot_general | solution.py:8
  164.3 9.9 %convolution_convert_fusion = bf16[896,8192]{1,0:T(8,128)(2,1)} fusion(bf16[8192,256]{1,0:T(8,128)(2,1)} %all-gather.3.cloned.1.call-done, f32[896,256]{1,0:T(8,128)S(1)} %fusion.4, f32[896,256]{1,0:T(8,128)S(1)} %fusion.5), kind=kOutput, calls=%fused_computation | convolution fusion | flops 3766812672 | bytes 20709376 | tf_op jit(solution)/shard_map/dot_general | solution.py:8
  174.2 72.2 %reduce-scatter.2.cloned.1.call-done = f32[512,256]{0,1:T(8,128)} async-done(((f32[8192,256]{0,1:T(8,128)}), f32[512,256]{0,1:T(8,128)}) %reduce-scatter.2.cloned.1.call-update) | async-done | bytes 524304 | tf_op jit(solution)/shard_map/reduce_scatter | solution.py:47
  246.4 1.1 convert_element_type.23
  247.4 0.8 copy.9
Async XLA Ops:
  7.2 53.6 %all-gather.5.cloned.1.call-start = ((), (), s32[]{:S(2)}) async-start(), calls=%async_computation.2 | async-start | bytes 4456448 | tf_op jit(solution)/shard_map/all_gather | solution.py:35
  7.9 104.0 %all-gather.3.cloned.1.call-start = ((), (), s32[]{:S(2)}) async-start(), calls=%async_computation.1 | async-start | bytes 4456448 | tf_op jit(solution)/shard_map/all_gather | solution.py:39
  8.6 237.7 %reduce-scatter.2.cloned.1.call-start = ((), (), s32[]{:S(2)}) async-start(), calls=%async_computation.3 | async-start | bytes 8912896 | tf_op jit(solution)/shard_map/reduce_scatter | solution.py:47
  60.8 10.7 %copy-start = (bf16[896,8192]{1,0:T(8,128)(2,1)S(1)}, bf16[896,8192]{1,0:T(8,128)(2,1)}, u32[]{:S(2)}) copy-start(bf16[896,8192]{1,0:T(8,128)(2,1)} %param.8) | copy-start | bytes 44040196
  60.8 12.0 %copy-start.1 = (bf16[8192,256]{1,0:T(8,128)(2,1)S(1)}, bf16[8192,256]{1,0:T(8,128)(2,1)}, u32[]{:S(2)}) copy-start(bf16[8192,256]{1,0:T(8,128)(2,1)} %all-gather.5.cloned.1.call-done) | copy-start | bytes 12582916
Sparse Core Ops, SparseCore 0:
  10.1 50.5 all-gather.4
  62.9 48.8 all-gather.2
  143.1 103.2 reduce-scatter.1
where the time goes:
time: 257 us; the launch traced here: 255 us
  waiting for transfers between devices  161 us (63%)
  matrix products  74.8 us (29%)
  between operations  13.8 us (5%)
  local copies, waits for them, and re-layouts  4.25 us (2%)
    reduce_scatter x1, waiting for transfers between devices, on_device(): lax.psum_scatter(terms, 'row', scatter_dimension=0, tiled=True)  72.2 us
    all_gather x1, waiting for transfers between devices, on_device(): block_in = lax.all_gather(layer_input, 'row', axis=0, tiled=True)  52.1 us
    all_gather x1, waiting for transfers between devices, on_device(): block_in = lax.all_gather(output_grad, 'row', axis=0, tiled=True)  35.1 us
    dot_general x3, matrix products, over_tokens(): lax.dot_general(first_mat, second_mat, (((1,), (1,)), ((), ())), preferre...  31.2 us
    dot_general x2, matrix products, over_hidden(): lax.dot_general(first_mat, second_mat, (((0,), (0,)), ((), ())), preferre...  20.6 us
    dot_general x1, matrix products, on_device(): jnp.dot(down_weight, block_in, preferred_element_type=jnp.float32)  10.5 us
    dot_general x1, matrix products, on_device(): jnp.dot(gate_weight, block_in, preferred_element_type=jnp.float32)  8.59 us
  transfers between devices with their start and end apart: 3, of which 3 were waited for; matrix products, arithmetic and copies ran while one was open for 17% of the time, Pallas kernels for 0%

commit v1 on v0

v1 whole, which is shorter than its diff:
```python
import functools

import jax
import jax.numpy as jnp
from jax import lax
from jax.experimental import pallas as pl
from jax.experimental.pallas import tpu as pltpu
from jax.sharding import PartitionSpec as P

MESH = pl.DeviceIdType.MESH
VMEM_LIMIT = 64 * 1000 * 1000


def over_tokens(first_mat, second_mat):
    return lax.dot_general(
        first_mat, second_mat, (((1,), (1,)), ((), ())), preferred_element_type=jnp.float32
    )


def nearest(rank, here, extent):
    low = jnp.minimum(here, extent - 1 - here)
    half = (rank + 1) // 2
    both = jnp.where(rank % 2 == 1, here + half, here - half)
    one = jnp.where(here < extent - 1 - here, rank, extent - 1 - rank)
    return jnp.where(rank <= 2 * low, both, one)


def place(zs, xs):
    me = lax.axis_index("row")
    core = me % 2
    x = (me // 2) % xs
    z = me // (2 * xs)
    return z, x, core


def chip_at(step, z, x, zs, xs):
    cz = nearest(step // xs, z, zs)
    cx = nearest(step % xs, x, xs)
    return cz, cx, cz * xs + cx


def greet(z, x, core, zs, xs):
    barrier = pltpu.get_barrier_semaphore()

    def hail(cz, cx, cc):
        pl.semaphore_signal(
            barrier, inc=1, device_id={"row": (cz * xs + cx) * 2 + cc}, device_id_type=MESH
        )

    hail(z, x, 1 - core)
    pl.when(z > 0)(lambda: hail(z - 1, x, core))
    pl.when(z < zs - 1)(lambda: hail(z + 1, x, core))
    pl.when(x > 0)(lambda: hail(z, x - 1, core))
    pl.when(x < xs - 1)(lambda: hail(z, x + 1, core))
    count = 1 + jnp.minimum(z, 1) + jnp.minimum(zs - 1 - z, 1)
    count = count + jnp.minimum(x, 1) + jnp.minimum(xs - 1 - x, 1)
    pl.semaphore_wait(barrier, count)


def forward_kernel(
    zs, xs, x_ref, dy_ref, wg_ref, wu_ref, wd_ref,
    hact_ref, ggp_ref, gup_ref, xg_ref, dyg_ref,
    held, wbuf, acc, send_sem, recv_sem, wsem, own_sem, out_sem,
):
    z, x, core = place(zs, xs)
    mine = z * xs + x
    chips = zs * xs
    rows, hidden = held.shape[3], acc.shape[1]
    width = 2 * rows
    tokens = held.shape[4]

    def weights(step, fn):
        _, _, chip = chip_at(step, z, x, zs, xs)
        cols = pl.ds(pl.multiple_of(chip * width, 128), width)
        slot = step % 2
        for n, ref in enumerate((wg_ref, wu_ref, wd_ref)):
            fn(pltpu.make_async_copy(ref.at[:, cols], wbuf.at[slot, n], wsem.at[slot, n]))

    weights(0, lambda c: c.start())
    own = [
        pltpu.make_async_copy(ref, held.at[mine, n, core], own_sem.at[n])
        for n, ref in enumerate((x_ref, dy_ref))
    ]
    for c in own:
        c.start()
    greet(z, x, core, zs, xs)
    for c in own:
        c.wait()

    def passing(step, fn):
        cz, cx, chip = chip_at(step, z, x, zs, xs)
        block = held.at[chip, :, core]

        def copy(tz, tx, tc, n):
            return lambda: fn(
                pltpu.make_async_remote_copy(
                    src_ref=block,
                    dst_ref=block,
                    send_sem=send_sem.at[n, chip],
                    recv_sem=recv_sem.at[chip, core],
                    device_id={"row": (tz * xs + tx) * 2 + tc},
                    device_id_type=MESH,
                )
            )

        pl.when((cx == x) & (cz <= z) & (z < zs - 1))(copy(z + 1, x, core, 0))
        pl.when((cx == x) & (cz >= z) & (z > 0))(copy(z - 1, x, core, 1))
        pl.when((cx <= x) & (x < xs - 1))(copy(z, x + 1, core, 2))
        pl.when((cx >= x) & (x > 0))(copy(z, x - 1, core, 3))
        copy(z, x, 1 - core, 4)()

    def arrive(step, which):
        _, _, chip = chip_at(step, z, x, zs, xs)
        block = held.at[chip, :, which]
        pltpu.make_async_copy(block, block, recv_sem.at[chip, which]).wait()

    passing(0, lambda c: c.start())
    acc[...] = jnp.zeros_like(acc)

    def body(step, carry):
        @pl.when(step + 1 < chips)
        def _():
            weights(step + 1, lambda c: c.start())
            arrive(step + 1, core)
            passing(step + 1, lambda c: c.start())

        arrive(step, 1 - core)
        weights(step, lambda c: c.wait())
        _, _, chip = chip_at(step, z, x, zs, xs)
        for n, ref in enumerate((xg_ref, dyg_ref)):
            pltpu.make_async_copy(held.at[chip, n], ref.at[chip], out_sem.at[n, chip]).start()
        slot = step % 2
        x_block = held[chip, 0].reshape(width, tokens)
        acc[0] += jnp.dot(wbuf[slot, 0], x_block, preferred_element_type=jnp.float32)
        acc[1] += jnp.dot(wbuf[slot, 1], x_block, preferred_element_type=jnp.float32)
        dy_block = held[chip, 1].reshape(width, tokens)
        acc[2] += jnp.dot(wbuf[slot, 2], dy_block, preferred_element_type=jnp.float32)
        return carry

    lax.fori_loop(0, chips, body, 0)

    part = 112 if hidden % 112 == 0 else hidden

    def finish(n, carry):
        at = pl.ds(pl.multiple_of(n * part, 16), part)
        gate_pre, up_pre, hidden_grad = acc[0, at], acc[1, at], acc[2, at]
        sig = jax.nn.sigmoid(gate_pre)
        act = gate_pre * sig
        hact_ref[at] = (act * up_pre).astype(jnp.bfloat16)
        ggp_ref[at] = (
            hidden_grad * up_pre * sig * (1.0 + gate_pre * (1.0 - sig))
        ).astype(jnp.bfloat16)
        gup_ref[at] = (hidden_grad * act).astype(jnp.bfloat16)
        return carry

    lax.fori_loop(0, hidden // part, finish, 0)

    def drain(step, carry):
        _, _, chip = chip_at(step, z, x, zs, xs)
        passing(step, lambda c: c.wait_send())
        for n, ref in enumerate((xg_ref, dyg_ref)):
            pltpu.make_async_copy(held.at[chip, n], ref.at[chip], out_sem.at[n, chip]).wait()
        return carry

    lax.fori_loop(0, chips, drain, 0)


def scatter_kernel(
    zs, xs, ggp_ref, gup_ref, wg_ref, wu_ref, out_ref,
    wbuf, part, core_out, core_in, line_out, x_in, z_in,
    wsem, core_send, core_recv, line_send, x_recv, z_recv,
):
    z, x, core = place(zs, xs)
    chips = zs * xs
    rows, tokens = out_ref.shape
    width = 2 * rows

    def chip_of(step):
        return chip_at(chips - 1 - step, z, x, zs, xs)

    def weights(step, fn):
        _, _, chip = chip_of(step)
        cols = pl.ds(pl.multiple_of(chip * width, 128), width)
        slot = step % 2
        for n, ref in enumerate((wg_ref, wu_ref)):
            fn(pltpu.make_async_copy(ref.at[:, cols], wbuf.at[slot, n], wsem.at[slot, n]))

    def to_core(chip):
        return pltpu.make_async_remote_copy(
            src_ref=core_out.at[chip],
            dst_ref=core_in.at[chip],
            send_sem=core_send.at[chip],
            recv_sem=core_recv.at[chip],
            device_id={"row": (z * xs + x) * 2 + 1 - core},
            device_id_type=MESH,
        )

    def line(chip, tz, tx, buf, sems, side):
        return pltpu.make_async_remote_copy(
            src_ref=line_out.at[chip],
            dst_ref=buf.at[side, chip],
            send_sem=line_send.at[chip],
            recv_sem=sems.at[side, chip],
            device_id={"row": (tz * xs + tx) * 2 + core},
            device_id_type=MESH,
        )

    def onward(cz, cx, chip, fn):
        pl.when(cx > x)(lambda: fn(line(chip, z, x + 1, x_in, x_recv, 0)))
        pl.when(cx < x)(lambda: fn(line(chip, z, x - 1, x_in, x_recv, 1)))
        pl.when((cx == x) & (cz > z))(lambda: fn(line(chip, z + 1, x, z_in, z_recv, 0)))
        pl.when((cx == x) & (cz < z))(lambda: fn(line(chip, z - 1, x, z_in, z_recv, 1)))

    weights(0, lambda c: c.start())
    greet(z, x, core, zs, xs)

    def make(step):
        slot = step % 2
        _, _, chip = chip_of(step)

        @pl.when(step + 1 < chips)
        def _():
            weights(step + 1, lambda c: c.start())

        weights(step, lambda c: c.wait())
        total = jnp.dot(ggp_ref[...], wbuf[slot, 0], preferred_element_type=jnp.float32)
        total += jnp.dot(gup_ref[...], wbuf[slot, 1], preferred_element_type=jnp.float32)
        part[slot] = total.T.reshape(2, rows, tokens)
        core_out[chip] = part[slot, 1 - core].astype(jnp.bfloat16)
        to_core(chip).start()

    def add(step):
        slot = step % 2
        cz, cx, chip = chip_of(step)
        to_core(chip).wait_recv()
        part[slot, core] += core_in[chip].astype(jnp.float32)

        def take(buf, sems, side):
            def run():
                block = buf.at[side, chip]
                pltpu.make_async_copy(block, block, sems.at[side, chip]).wait()
                part[slot, core] += buf[side, chip].astype(jnp.float32)

            return run

        pl.when((cx >= x) & (x > 0))(take(x_in, x_recv, 0))
        pl.when((cx <= x) & (x < xs - 1))(take(x_in, x_recv, 1))
        pl.when((cx == x) & (cz >= z) & (z > 0))(take(z_in, z_recv, 0))
        pl.when((cx == x) & (cz <= z) & (z < zs - 1))(take(z_in, z_recv, 1))
        line_out[chip] = part[slot, core].astype(jnp.bfloat16)
        onward(cz, cx, chip, lambda c: c.start())

    make(0)

    def body(step, carry):
        make(step)
        add(step - 1)
        return carry

    lax.fori_loop(1, chips, body, 0)
    add(chips - 1)
    out_ref[...] = line_out[z * xs + x]

    def drain(step, carry):
        cz, cx, chip = chip_of(step)
        to_core(chip).wait_send()
        onward(cz, cx, chip, lambda c: c.wait_send())
        return carry

    lax.fori_loop(0, chips, drain, 0)


def on_device(zs, xs, layer_input, output_grad, gate_weight, up_weight, down_weight):
    chips = zs * xs
    rows, tokens = layer_input.shape
    hidden, features = gate_weight.shape
    width = 2 * rows
    bf16, f32 = jnp.bfloat16, jnp.float32
    anywhere = pl.BlockSpec(memory_space=pl.ANY)
    vmem = pl.BlockSpec(memory_space=pltpu.VMEM)
    DMA = pltpu.SemaphoreType.DMA
    small = jax.ShapeDtypeStruct((hidden, tokens), bf16)
    whole = jax.ShapeDtypeStruct((chips, 2, rows, tokens), bf16)
    hidden_act, ggp, gup, xg, dyg = pl.pallas_call(
        functools.partial(forward_kernel, zs, xs),
        out_shape=(small, small, small, whole, whole),
        in_specs=[anywhere] * 5,
        out_specs=(vmem, vmem, vmem, anywhere, anywhere),
        scratch_shapes=[
            pltpu.VMEM((chips, 2, 2, rows, tokens), bf16),
            pltpu.VMEM((2, 3, hidden, width), bf16),
            pltpu.VMEM((3, hidden, tokens), f32),
            DMA((5, chips)),
            DMA((chips, 2)),
            DMA((2, 3)),
            DMA((2,)),
            DMA((2, chips)),
        ],
        compiler_params=pltpu.CompilerParams(
            collective_id=0, has_side_effects=True, vmem_limit_bytes=VMEM_LIMIT
        ),
        name="gather_forward",
    )(layer_input, output_grad, gate_weight, up_weight, down_weight)
    input_grad = pl.pallas_call(
        functools.partial(scatter_kernel, zs, xs),
        out_shape=jax.ShapeDtypeStruct((rows, tokens), bf16),
        in_specs=[vmem, vmem, anywhere, anywhere],
        out_specs=vmem,
        scratch_shapes=[
            pltpu.VMEM((2, 2, hidden, width), bf16),
            pltpu.VMEM((2, 2, rows, tokens), f32),
            pltpu.VMEM((chips, rows, tokens), bf16),
            pltpu.VMEM((chips, rows, tokens), bf16),
            pltpu.VMEM((chips, rows, tokens), bf16),
            pltpu.VMEM((2, chips, rows, tokens), bf16),
            pltpu.VMEM((2, chips, rows, tokens), bf16),
            DMA((2, 2)),
            DMA((chips,)),
            DMA((chips,)),
            DMA((chips,)),
            DMA((2, chips)),
            DMA((2, chips)),
        ],
        compiler_params=pltpu.CompilerParams(
            collective_id=1, has_side_effects=True, vmem_limit_bytes=VMEM_LIMIT
        ),
        name="scatter_input_grad",
    )(ggp.T, gup.T, gate_weight, up_weight)
    block_in = xg.reshape(features, tokens)
    block_dy = dyg.reshape(features, tokens)
    down_grad = over_tokens(hidden_act, block_dy).astype(bf16)
    gate_grad = over_tokens(ggp, block_in).astype(bf16)
    up_grad = over_tokens(gup, block_in).astype(bf16)
    return (input_grad, gate_grad, up_grad, down_grad)


def solution(mesh):
    row = mesh.shape["row"]
    xs = 2 if row <= 16 else 4
    zs = row // (2 * xs)
    return jax.shard_map(
        functools.partial(on_device, zs, xs),
        mesh=mesh,
        in_specs=(
            P("row", "groups"),
            P("row", "groups"),
            P(("groups", "row"), None),
            P(("groups", "row"), None),
            P(("groups", "row"), None),
        ),
        out_specs=(
            P("row", "groups"),
            P(("groups", "row"), None),
            P(("groups", "row"), None),
            P(("groups", "row"), None),
        ),
        check_vma=False,
    )
```

time: 257 us -> 154 us (0.60)
  waiting for transfers between devices: 161 us -> 0 us
  Pallas kernels: 0 us -> 119 us
  matrix products: 74.8 us -> 29.4 us
  between operations: 13.8 us -> 0.67 us
    pallas_call x0 -> x2, Pallas kernels: none -> 119 us  [the longest x1 62 us: on_device(): pl.pallas_call(functools.partial(forward_kernel, zs, xs), out_shape=(smal...]
    all_gather x2 -> x0, waiting for transfers between devices: 87.2 us -> none  [the longest x1 52.1 us: on_device(): block_in = lax.all_gather(layer_input, 'row', axis=0, tiled=True)]
    reduce_scatter x1 -> x0, waiting for transfers between devices: 72.2 us -> none  [on_device(): lax.psum_scatter(terms, 'row', scatter_dimension=0, tiled=True)]
    dot_general x5 -> x0, matrix products: 43.6 us -> none  [the longest x2 20.6 us: over_hidden(): lax.dot_general(first_mat, second_mat, (((0,), (0,)), ((), ())), preferre...]
    pallas_call x0 -> x2, local copies, waits for them, and re-layouts: none -> 3.98 us  [on_device(): pl.pallas_call(functools.partial(forward_kernel, zs, xs), out_shape=(smal...]
    unnamed x5 -> x9, local copies, waits for them, and re-layouts: 4.25 us -> 0.72 us
  transfers between devices with their start and end apart: 3 -> 0, of which waited for: 3 -> 0; matrix products, arithmetic and copies ran while one was open for 17% -> 0% of each run, Pallas kernels for 0% -> 0%
where the time goes in v1:
time: 154 us
  Pallas kernels  119 us (77%)
  matrix products  29.4 us (19%)
  local copies, waits for them, and re-layouts  4.7 us (3%)
    pallas_call x1, Pallas kernels, on_device(): pl.pallas_call(functools.partial(forward_kernel, zs, xs), out_shape=(smal...  62 us
    pallas_call x1, Pallas kernels, on_device(): pl.pallas_call(functools.partial(scatter_kernel, zs, xs), out_shape=jax.S...  57 us
    dot_general x3, matrix products, over_tokens(): lax.dot_general(first_mat, second_mat, (((1,), (1,)), ((), ())), preferre...  29.4 us
    pallas_call x2, local copies, waits for them, and re-layouts, on_device(): pl.pallas_call(functools.partial(forward_kernel, zs, xs), out_shape=(smal...  3.98 us

profile of v1, /device:TPU:14, one launch (start us, length us, event | category | flops | bytes accessed | tf_op | source)
XLA Modules:
  0.0 153.8 jit_solution(8575500066687785284)
XLA Ops:
  0.6 62.0 %gather_forward.1 = (bf16[896,256]{1,0:T(8,128)(2,1)}, bf16[896,256]{1,0:T(8,128)(2,1)}, bf16[896,256]{1,0:T(8,128)(2,1)}, bf16[8,2,512,256]{3,2,1,0:T(8,128)(2,1)}, bf16[8,2,512,256]{3,2,1,0:T(8,128)(2,1)}) custom-call(bf16[512,256]{1,0:T(8,128)(2,1)} %x_ref.1, bf16[512,256]{1,0:T(8,128)(2,1)} %dy_ref.1, bf16[896,8192]{1,0:T(8,128)(2,1)} %wg_ref.3, ...), custom_call_target="tpu_custom_call" | custom-call | tf_op jit(solution)/shard_map/gather_forward/pallas_call | solution.py:284
  62.6 2.0 %copy.9 = bf16[896,256]{0,1:T(8,128)(2,1)} copy(bf16[896,256]{1,0:T(8,128)(2,1)} %get-tuple-element.9) | data formatting | bytes 917504 | tf_op jit(solution)/shard_map/gather_forward/pallas_call | solution.py:284
  64.6 2.0 %copy.10 = bf16[896,256]{0,1:T(8,128)(2,1)} copy(bf16[896,256]{1,0:T(8,128)(2,1)} %get-tuple-element.10) | data formatting | bytes 917504 | tf_op jit(solution)/shard_map/gather_forward/pallas_call | solution.py:284
  66.6 0.0 copy-start.1
  66.6 57.0 %scatter_input_grad.1 = bf16[512,256]{1,0:T(8,128)(2,1)} custom-call(bf16[256,896]{1,0:T(8,128)(2,1)} %bitcast.13, bf16[256,896]{1,0:T(8,128)(2,1)} %bitcast.14, bf16[896,8192]{1,0:T(8,128)(2,1)} %wg_ref.3, bf16[896,8192]{1,0:T(8,128)(2,1)} %wu_ref.3), custom_call_target="tpu_custom_call" | custom-call | tf_op jit(solution)/shard_map/scatter_input_grad/pallas_call | solution.py:304
  123.6 0.0 copy-done.1
  123.6 0.0 copy-start
  123.6 9.8 %convolution_convert_fusion.1 = bf16[896,8192]{1,0:T(8,128)(2,1)} fusion(bf16[896,256]{1,0:T(8,128)(2,1)S(1)} %copy-done.1, bf16[8192,256]{1,0:T(8,128)(2,1)} %bitcast.10), kind=kOutput, calls=%fused_computation.1 | convolution fusion | flops 3765436416 | bytes 19333120 | tf_op jit(solution)/shard_map/dot_general | solution.py:15
  133.4 0.0 copy-done
  133.5 0.0 copy-start.3
  133.5 9.8 %convolution_convert_fusion.2 = bf16[896,8192]{1,0:T(8,128)(2,1)} fusion(bf16[896,256]{1,0:T(8,128)(2,1)S(1)} %copy-done, bf16[8192,256]{1,0:T(8,128)(2,1)} %bitcast.11), kind=kOutput, calls=%fused_computation.2 | convolution fusion | flops 3765436416 | bytes 19333120 | tf_op jit(solution)/shard_map/dot_general | solution.py:15
  143.3 0.0 copy-done.3
  143.3 0.0 copy-start.2
  143.3 9.8 %convolution_convert_fusion = bf16[896,8192]{1,0:T(8,128)(2,1)} fusion(bf16[896,256]{1,0:T(8,128)(2,1)S(1)} %copy-done.3, bf16[8192,256]{1,0:T(8,128)(2,1)} %bitcast.12), kind=kOutput, calls=%fused_computation | convolution fusion | flops 3765436416 | bytes 19333120 | tf_op jit(solution)/shard_map/dot_general | solution.py:15
  153.1 0.0 copy-done.2
  153.1 0.7 copy.12
Async XLA Ops:
  66.6 57.0 %copy-start.1 = (bf16[896,256]{1,0:T(8,128)(2,1)S(1)}, bf16[896,256]{1,0:T(8,128)(2,1)}, u32[]{:S(2)}) copy-start(bf16[896,256]{1,0:T(8,128)(2,1)} %get-tuple-element.10) | copy-start | bytes 1376260
  123.6 9.8 %copy-start = (bf16[896,256]{1,0:T(8,128)(2,1)S(1)}, bf16[896,256]{1,0:T(8,128)(2,1)}, u32[]{:S(2)}) copy-start(bf16[896,256]{1,0:T(8,128)(2,1)} %get-tuple-element.9) | copy-start | bytes 1376260
  133.5 9.8 %copy-start.3 = (bf16[896,256]{1,0:T(8,128)(2,1)S(1)}, bf16[896,256]{1,0:T(8,128)(2,1)}, u32[]{:S(2)}) copy-start(bf16[896,256]{1,0:T(8,128)(2,1)} %get-tuple-element.12) | copy-start | bytes 1376260
  143.3 9.8 %copy-start.2 = (bf16[512,256]{1,0:T(8,128)(2,1)S(1)}, bf16[512,256]{1,0:T(8,128)(2,1)}, u32[]{:S(2)}) copy-start(bf16[512,256]{1,0:T(8,128)(2,1)} %scatter_input_grad.1) | copy-start | bytes 786436
